TPU v7x, 32 devices: a whole 2x2x4 slice. The times are simulated.
32 devices in a mesh: grp: 4 (over y, x), space: 8 (over z, core).
Axes of the slice: x: 2, y: 2, z: 4, core: 2. Of those that a mesh axis runs over, the one named last changes fastest.
Arguments:
- features: bfloat16 [4, 128, 128, 128], P('grp', 'space'), may hold values from -6 to 6
- weights: bfloat16 [27, 128, 128], replicated, may hold values from -0.109375 to 0.109375
- cotangent: bfloat16 [4, 128, 128, 128], P('grp', 'space'), may hold values from -6 to 6
- kernel_map: int32 [4, 128, 27], P('grp', 'space'), may hold values from -1 to 127, as said below
- counts: int32 [4, 8], P('grp', 'space'), may hold values from 4 to 16
Outputs:
- output: bfloat16 [4, 128, 128, 128], P('grp', 'space')
- input_grad: bfloat16 [4, 128, 128, 128], P('grp', 'space')
- weight_grad: float32 [3456, 128], P('space')
Inputs may be any that keep to these rules, and one draw needn't show every extreme that they name: `kernel_map`: the centre offset k = 27 div 2 maps every block to itself. Otherwise an entry for an output block b on slab d = b div 16 is -1 or lies in [d * 16 - 4, (d + 1) * 16 + 4) within the sample. The live blocks of a device are its first counts slots.
All inputs are finite; a program needn't handle non-finite values.
Results may differ from a plain program's by a relative error of at most 0.005.
Values may be sent and summed in bfloat16 or wider, within the bound.
A program may use at most 64 MiB of HBM per device.

v0:
```python
import functools

import jax
import jax.numpy as jnp
from jax import lax
from jax.experimental import pallas as pl
from jax.experimental.pallas import tpu as pltpu
from jax.sharding import PartitionSpec as P

H = 4
BF16, F32 = jnp.bfloat16, jnp.float32
VMEM = pl.BlockSpec(memory_space=pltpu.VMEM)
FAR = pl.BlockSpec(memory_space=pl.ANY)
SMEM = pl.BlockSpec(memory_space=pltpu.SMEM)


def input_grad_kernel(where, counts, block_map, cot, feat, w, idx, top, rims, own, acc):
    slots = cot.shape[0]
    offsets = block_map.shape[1]
    cin = acc.shape[2]
    live = counts[0, 0]
    first = where[0] * slots - H
    nowhere = slots + 2 * H

    def clear(i, carry):
        acc[i] = jnp.zeros(acc.shape[1:], F32)
        return carry

    lax.fori_loop(0, acc.shape[0], clear, 0)

    height = cot.shape[1]
    both = 4 if slots % 4 == 0 else 2

    def body(i, carry):
        g = jnp.concatenate([cot[i * both + h] for h in range(both)], axis=0)
        for k in range(0, offsets, 2):
            n = min(2, offsets - k)
            term = lax.dot_general(
                g, w[k * cin : (k + n) * cin], (((1,), (1,)), ((), ())), preferred_element_type=F32
            )
            for h in range(both):
                b = i * both + h
                for j in range(n):
                    source = block_map[b, k + j]
                    local = source - first
                    dead = jnp.logical_and(local - H >= live, local < slots + H)
                    skip = jnp.logical_or(jnp.logical_or(source < 0, b >= live), dead)
                    a = jnp.where(skip, nowhere, local)
                    idx[b, k + j] = a
                    acc[a] = acc[a] + term[h * height : (h + 1) * height, j * cin : (j + 1) * cin]
        return carry

    lax.fori_loop(0, slots // both, body, 0)
    for i in range(H):
        alive = jnp.where(slots - H + i < live, 1.0, 0.0).astype(BF16)
        top[i] = feat[slots - H + i] * alive
        rims[0, i] = acc[i].astype(BF16)
        rims[1, i] = acc[H + slots + i].astype(BF16)
    for i in range(slots):
        own[i] = acc[H + i]


def window_start(g, groups, unit, rows):
    return pl.multiple_of(g * unit - (g // (groups - 1)) * (groups * unit - rows), 16)


def main_kernel(
    groups, space, unit, rows, padded,
    idx, top, feat, rims, w_far, cot_far,
    out, below, above, wg,
    w, cot, ext, turned, flat, part, r0, p1, r1, p2, r2, r3,
    sl, sh, qh, sr, qr, s0, q0, s1, q1, s2, q2, s3, q3,
):
    g = lax.axis_index("grp")
    s = lax.axis_index("space")
    half = space // 2
    z, c = s // 2, s % 2
    slots, height, cin = feat.shape
    offsets = idx.shape[1]
    partner = (g, z * 2 + (1 - c))
    grp_peers = [((g + d) % groups, s) for d in range(1, groups)]
    z_peers = [(g, ((z + d) % half) * 2 + c) for d in range(1, half)]

    barrier = pltpu.get_barrier_semaphore()
    fixed = [partner] + grp_peers + z_peers
    for peer in fixed:
        pl.semaphore_signal(barrier, inc=1, device_id=peer, device_id_type=pl.DeviceIdType.MESH)
    across = s - 1 + 2 * c
    has_across = jnp.logical_and(across >= 0, across < space)

    @pl.when(has_across)
    def _():
        pl.semaphore_signal(barrier, inc=1, device_id=(g, across), device_id_type=pl.DeviceIdType.MESH)

    def turn(i):
        turned[i] = ext[i].T

    load_feat = pltpu.make_async_copy(feat, ext.at[pl.ds(H, slots)], sl.at[2])
    load_feat.start()
    load_cot = pltpu.make_async_copy(cot_far, cot, sl.at[0])
    load_w = pltpu.make_async_copy(w_far, w, sl.at[1])
    load_cot.start()
    load_w.start()
    pl.semaphore_wait(barrier, len(fixed) + has_across.astype(jnp.int32))

    def remote(src, dst, send, recv, peer):
        return pltpu.make_async_remote_copy(
            src_ref=src, dst_ref=dst, send_sem=send, recv_sem=recv,
            device_id=peer, device_id_type=pl.DeviceIdType.MESH,
        )

    halo_down = remote(feat.at[pl.ds(0, H)], ext.at[pl.ds(H + slots, H)], sh.at[0], qh.at[0], (g, s - 1))
    halo_up = remote(top, ext.at[pl.ds(0, H)], sh.at[1], qh.at[1], (g, s + 1))
    down = remote(rims.at[0], above, sr.at[0], qr.at[0], (g, s - 1))
    up = remote(rims.at[1], below, sr.at[1], qr.at[1], (g, s + 1))
    has_down, has_up = s > 0, s < space - 1

    @pl.when(has_down)
    def _():
        halo_down.start()

    @pl.when(has_up)
    def _():
        halo_up.start()

    zero = jnp.zeros((height, cin), BF16)
    ext[2 * H + slots] = zero
    turned[2 * H + slots] = zero
    load_feat.wait()
    for i in range(slots):
        turn(H + i)

    @pl.when(has_down)
    def _():
        halo_up.wait_recv()
        for i in range(H):
            turn(i)

    @pl.when(jnp.logical_not(has_down))
    def _():
        for i in range(H):
            ext[i] = zero
            turned[i] = zero

    @pl.when(has_up)
    def _():
        halo_down.wait_recv()
        for i in range(H):
            turn(H + slots + i)

    @pl.when(jnp.logical_not(has_up))
    def _():
        for i in range(H):
            ext[H + slots + i] = zero
            turned[H + slots + i] = zero

    @pl.when(has_down)
    def _():
        down.start()

    @pl.when(has_up)
    def _():
        up.start()

    load_cot.wait()
    group = 3 if offsets % 3 == 0 else 1
    steps = offsets // group
    span = group * cin
    direct = rows == padded

    def weight_step(i, carry):
        lhs = [
            jnp.concatenate([turned[idx[b, i * group + j]] for b in range(slots)], axis=1)
            for j in range(group)
        ]
        got = jnp.dot(jnp.concatenate(lhs, axis=0), cot[...], preferred_element_type=F32)
        at = pl.ds(pl.multiple_of(i * span, span), span)
        if direct:
            part[at, :] = got
        else:
            flat[at, :] = got
        return carry

    pairs = slots // 2

    def forward(i, carry):
        lhs = [
            jnp.concatenate([ext[idx[2 * i + j, k]] for k in range(offsets)], axis=1)
            for j in range(2)
        ]
        got = jnp.dot(jnp.concatenate(lhs, axis=0), w[...], preferred_element_type=F32)
        for j in range(2):
            out[2 * i + j] = got[j * height : (j + 1) * height].astype(BF16)
        return carry

    def piece(p):
        return pl.ds(pl.multiple_of(p * padded, 16), padded)

    done = 0
    if not direct:
        lax.fori_loop(0, steps, weight_step, 0)
        done = steps
        for p in range(space):
            part[p * padded : p * padded + rows, :] = flat[p * rows : (p + 1) * rows, :]
            part[p * padded + rows : (p + 1) * padded, :] = jnp.zeros((padded - rows, part.shape[1]), F32)

    here = window_start(g, groups, unit, padded)
    copies0, copies1 = [], []
    copies2, copies3 = [], []
    for t in range(half + 4):
        if t < half:
            need = max(done, -(-(t + 1) * 2 * rows // span))
            if need > done:
                lax.fori_loop(done, need, weight_step, 0)
                done = need
            copies0.append(remote(part.at[piece(2 * t + 1 - c)], r0.at[t], s0.at[t], q0.at[t], partner))
            copies0[t].start()
        else:
            q = t - half
            if q == 0:
                load_w.wait()
            lax.fori_loop(q * pairs // 4, (q + 1) * pairs // 4, forward, 0)
        i = t - 1
        if 0 <= i < half:
            copies0[i].wait_recv()
            p1[i] = (part[piece(2 * i + c), :] + r0[i]).astype(BF16)
            copies1.append([])
            for d in range(1, groups):
                there = window_start((g + d) % groups, groups, unit, padded)
                copies1[i].append(
                    remote(p1.at[i, pl.ds(there, unit)], r1.at[i, d - 1], s1.at[i, d - 1], q1.at[i, d - 1], grp_peers[d - 1])
                )
                copies1[i][-1].start()
        i = t - 2
        if 0 <= i < half:
            total = p1[i, pl.ds(here, unit), :].astype(F32)
            for d in range(1, groups):
                copies1[i][d - 1].wait_recv()
                total = total + r1[i, d - 1].astype(F32)
            p2[i] = total.astype(BF16)
            copies2.append(remote(p2.at[i], r2.at[z], s2.at[i], q2.at[z], (g, 2 * i + c)))

            @pl.when(z != i)
            def _(i=i):
                copies2[i].start()

        if t == half + 2:
            r2[z] = p2[z]
            total = jnp.zeros((unit, wg.shape[1]), F32)
            for i in range(half):

                @pl.when(z != i)
                def _(i=i):
                    remote(p2.at[i], r2.at[i], s2.at[i], q2.at[i], (g, 2 * i + c)).wait_recv()

            for i in range(half):
                total = total + r2[i].astype(F32)
            r3[0] = total.astype(BF16)
            for d in range(1, groups):
                copies3.append(remote(r3.at[0], r3.at[d], s3.at[d - 1], q3.at[d - 1], grp_peers[d - 1]))
                copies3[-1].start()

    for copy in copies3:
        copy.wait_recv()
    for j in range(groups):
        at = min(j * unit, padded - unit)
        wg[at : at + unit, :] = r3[(g - j + groups) % groups].astype(F32)

    @pl.when(has_down)
    def _():
        up.wait_recv()
        halo_down.wait_send()
        down.wait_send()

    @pl.when(has_up)
    def _():
        down.wait_recv()
        halo_up.wait_send()
        up.wait_send()

    for copy in copies0 + sum(copies1, []) + copies3:
        copy.wait_send()
    for i in range(half):

        @pl.when(z != i)
        def _(i=i):
            copies2[i].wait_send()


def finish_kernel(
    space, where, counts, raw_far, own_far, below_far, above_far, wg_far, out_far, ig_far, wg_out,
    raw, own, below, above, wg_in, out, ig, wg, load, store,
):
    slots = raw.shape[0]
    device = where[0]
    parts = slots // H
    chunk = [pl.ds(q * H, H) for q in range(parts)]
    copy = pltpu.make_async_copy
    edges = [copy(below_far, below, load.at[2 * parts]), copy(above_far, above, load.at[2 * parts + 1])]
    sums = copy(wg_far, wg_in, load.at[2 * parts + 2])
    owns = [copy(own_far.at[chunk[q]], own.at[chunk[q]], load.at[q]) for q in range(parts)]
    raws = [copy(raw_far.at[chunk[q]], raw.at[chunk[q]], load.at[parts + q]) for q in range(parts)]
    for q in range(parts):
        owns[q].start()
        raws[q].start()
        if q == 0:
            for edge in edges:
                edge.start()
    sums.start()
    stores = []
    for q in range(parts):
        owns[q].wait()
        raws[q].wait()
        if q == 0:
            for edge in edges:
                edge.wait()
        for i in range(q * H, (q + 1) * H):
            alive = jnp.where(i < counts[0, 0], 1.0, 0.0).astype(F32)
            value = own[i]
            if i < H:
                value = value + jnp.where(device > 0, below[i].astype(F32), 0.0)
            if i >= slots - H:
                value = value + jnp.where(device < space - 1, above[i - slots + H].astype(F32), 0.0)
            ig[i] = (value * alive).astype(BF16)
            out[i] = raw[i] * alive.astype(BF16)
        stores.append(copy(ig.at[chunk[q]], ig_far.at[chunk[q]], store.at[q]))
        stores.append(copy(out.at[chunk[q]], out_far.at[chunk[q]], store.at[parts + q]))
        stores[-2].start()
        stores[-1].start()
    sums.wait()
    wg[...] = wg_in[: wg.shape[0], :]
    stores.append(copy(wg, wg_out, store.at[2 * parts]))
    stores[-1].start()
    for item in stores:
        item.wait()


def per_device(features, weights, cotangent, kernel_map, counts):
    voxels = features[0]
    slots, height, cin = voxels.shape
    offsets, _, cout = weights.shape
    space = lax.axis_size("space")
    groups = lax.axis_size("grp")
    device = lax.axis_index("space")
    position = device.astype(jnp.int32).reshape(1)
    nowhere = slots + 2 * H
    flat_w = weights.reshape(offsets * cin, cout)

    idx, top, rims, own = pl.pallas_call(
        input_grad_kernel,
        out_shape=(
            jax.ShapeDtypeStruct((slots, offsets), jnp.int32),
            jax.ShapeDtypeStruct((H, height, cin), BF16),
            jax.ShapeDtypeStruct((2, H, height, cin), BF16),
            jax.ShapeDtypeStruct((slots, height, cin), F32),
        ),
        in_specs=[SMEM, SMEM, SMEM, VMEM, VMEM, VMEM],
        out_specs=(SMEM, VMEM, VMEM, VMEM),
        scratch_shapes=[pltpu.VMEM((nowhere + 1, height, cin), F32)],
        name="input_grad",
    )(position, counts, kernel_map[0], cotangent[0], voxels, flat_w)

    half = space // 2
    rows = offsets * cin // space
    padded = -(-rows // 16) * 16
    unit = -(-padded // (16 * groups)) * 16
    dma = pltpu.SemaphoreType.DMA
    rim = jax.ShapeDtypeStruct((H, height, cin), BF16)
    output, below, above, wg = pl.pallas_call(
        functools.partial(main_kernel, groups, space, unit, rows, padded),
        out_shape=(
            jax.ShapeDtypeStruct((slots, height, cout), BF16),
            rim,
            rim,
            jax.ShapeDtypeStruct((padded, cout), F32),
        ),
        in_specs=[SMEM] + [FAR] * 5,
        out_specs=(VMEM,) * 4,
        scratch_shapes=[
            pltpu.VMEM((offsets * cin, cout), BF16),
            pltpu.VMEM((slots * height, cout), BF16),
            pltpu.VMEM((nowhere + 1, height, cin), BF16),
            pltpu.VMEM((nowhere + 1, cin, height), BF16),
            pltpu.VMEM((offsets * cin if rows != padded else 8, cout), F32),
            pltpu.VMEM((space * padded, cout), F32),
            pltpu.VMEM((half, padded, cout), F32),
            pltpu.VMEM((half, padded, cout), BF16),
            pltpu.VMEM((half, groups - 1, unit, cout), BF16),
            pltpu.VMEM((half, unit, cout), BF16),
            pltpu.VMEM((half, unit, cout), BF16),
            pltpu.VMEM((groups, unit, cout), BF16),
            dma((3,)),
            dma((2,)), dma((2,)),
            dma((2,)), dma((2,)),
            dma((half,)), dma((half,)),
            dma((half, groups - 1)), dma((half, groups - 1)),
            dma((half,)), dma((half,)),
            dma((groups - 1,)), dma((groups - 1,)),
        ],
        compiler_params=pltpu.CompilerParams(collective_id=0, has_side_effects=True),
        name="main",
    )(idx, top, voxels, rims, flat_w, cotangent[0].reshape(slots * height, cout))
    output, input_grad, wg = pl.pallas_call(
        functools.partial(finish_kernel, space),
        out_shape=(
            jax.ShapeDtypeStruct((slots, height, cout), BF16),
            jax.ShapeDtypeStruct((slots, height, cin), BF16),
            jax.ShapeDtypeStruct((rows, cout), F32),
        ),
        in_specs=[SMEM, SMEM] + [FAR] * 5,
        out_specs=(FAR,) * 3,
        scratch_shapes=[
            pltpu.VMEM((slots, height, cout), BF16),
            pltpu.VMEM((slots, height, cin), F32),
            pltpu.VMEM((H, height, cin), BF16),
            pltpu.VMEM((H, height, cin), BF16),
            pltpu.VMEM((padded, cout), F32),
            pltpu.VMEM((slots, height, cout), BF16),
            pltpu.VMEM((slots, height, cin), BF16),
            pltpu.VMEM((rows, cout), F32),
            dma((2 * (slots // H) + 3,)),
            dma((2 * (slots // H) + 1,)),
        ],
        name="finish",
    )(position, counts, output, own, below, above, wg)
    return output[None], input_grad[None], wg


def solution(mesh):
    in_specs = (
        P("grp", "space", None, None),
        P(),
        P("grp", "space", None, None),
        P("grp", "space", None),
        P("grp", "space"),
    )
    out_specs = (P("grp", "space", None, None), P("grp", "space", None, None), P("space", None))
    return jax.shard_map(
        per_device, mesh=mesh, in_specs=in_specs, out_specs=out_specs, check_vma=False
    )
```

profile of v0, /device:TPU:0, one launch (start us, length us, event | category | flops | bytes accessed | tf_op | source)
XLA Modules:
  0.0 40.6 jit_solution(2349839651449071921)
XLA Ops:
  1.3 7.8 %input_grad.1 = (s32[16,27]{1,0:T(8,128)}, bf16[4,128,128]{2,1,0:T(8,128)(2,1)}, bf16[2,4,128,128]{3,2,1,0:T(8,128)(2,1)}, f32[16,128,128]{2,1,0:T(8,128)}) custom-call(s32[1]{0:T(128)} %bitcast.where, s32[1,1]{1,0:T(1,128)S(6)} %copy.8.counts, s32[16,27]{1,0:T(8,128)} %bitcast.14, bf16[16,128,128]{2,1,0:T(8,128)(2,1)} %bitcast.10, ...), custom_call_target="tpu_custom_call" | custom-call | tf_op jit(solution)/shard_map/input_grad/pallas_call | solution.py:349
  9.1 29.1 %main.1 = (bf16[16,128,128]{2,1,0:T(8,128)(2,1)}, bf16[4,128,128]{2,1,0:T(8,128)(2,1)}, bf16[4,128,128]{2,1,0:T(8,128)(2,1)}, f32[432,128]{1,0:T(8,128)}) custom-call(s32[16,27]{1,0:T(8,128)} %get-tuple-element.14.idx, bf16[4,128,128]{2,1,0:T(8,128)(2,1)} %get-tuple-element.15.top, bf16[16,128,128]{2,1,0:T(8,128)(2,1)} %bitcast.13, ...), custom_call_target="tpu_custom_call" | custom-call | tf_op jit(solution)/shard_map/main/pallas_call | solution.py:369
  38.1 2.5 %finish.1 = (bf16[16,128,128]{2,1,0:T(8,128)(2,1)}, bf16[16,128,128]{2,1,0:T(8,128)(2,1)}, f32[432,128]{1,0:T(8,128)}) custom-call(s32[1]{0:T(128)} %bitcast.where, s32[1,1]{1,0:T(1,128)S(6)} %copy.8.counts, bf16[16,128,128]{2,1,0:T(8,128)(2,1)} %get-tuple-element.17.raw_far, f32[16,128,128]{2,1,0:T(8,128)} %get-tuple-element.18.own_far, ...), custom_call_target="tpu_custom_call" | custom-call | tf_op jit(solution)/shard_map/finish/pallas_call | solution.py:403
where the time goes:
time: 40.8 us; the launch traced here: 40.6 us
  Pallas kernels  39.3 us (96%)
  between operations  1.3 us (3%)
    pallas_call x1, Pallas kernels, per_device(): pl.pallas_call(functools.partial(main_kernel, groups, space, unit, rows,...  29.1 us
    pallas_call x1, Pallas kernels, per_device(): pl.pallas_call(input_grad_kernel, out_shape=(jax.ShapeDtypeStruct((slots,...  7.76 us
    pallas_call x1, Pallas kernels, per_device(): pl.pallas_call(functools.partial(finish_kernel, space), out_shape=(jax.Sh...  2.45 us

commit v1 on v0

v1 whole, which is shorter than its diff:
```python
import functools

import jax
import jax.numpy as jnp
from jax import lax
from jax.experimental import pallas as pl
from jax.experimental.pallas import tpu as pltpu
from jax.sharding import PartitionSpec as P

H = 4
WIDE = 2 * H
SPAN = 7
DEPTH = 4
BF16, F32 = jnp.bfloat16, jnp.float32
VMEM = pl.BlockSpec(memory_space=pltpu.VMEM)
FAR = pl.BlockSpec(memory_space=pl.ANY)
SMEM = pl.BlockSpec(memory_space=pltpu.SMEM)


def window_start(g, groups, unit, rows):
    return pl.multiple_of(g * unit - (g // (groups - 1)) * (groups * unit - rows), 16)


def main_kernel(
    groups, space, unit, rows, padded, piped,
    counts, block_map, feat, w_far, cot_far,
    out_far, ig_far, wg_far,
    w, cot, turned, blocks, ext, top, edge, fin, wg, tab, idx,
    flat, part, r0, p1, r1, p2, r2, r3,
    sl, so, sh, qh, sr, qr, s0, q0, s1, q1, s2, q2, s3, q3,
):
    g = lax.axis_index("grp")
    s = lax.axis_index("space")
    half = space // 2
    z, c = s // 2, s % 2
    slots, height, cin = feat.shape
    offsets = block_map.shape[1]
    near = slots + 2 * H
    empty = slots * offsets
    base = empty + 1
    live = counts[0, 0]
    partner = (g, z * 2 + (1 - c))
    grp_peers = [((g + d) % groups, s) for d in range(1, groups)]
    z_peers = [(g, ((z + d) % half) * 2 + c) for d in range(1, half)]
    copy = pltpu.make_async_copy

    load_top = copy(feat.at[pl.ds(slots - H, H)], top, sl.at[4])
    load_cot = copy(cot_far, cot, sl.at[0])
    load_w = copy(w_far, w.at[pl.ds(offsets, offsets)], sl.at[1])
    load_feat = copy(feat, ext.at[pl.ds(1 + H, slots)], sl.at[2])
    load_top.start()
    load_cot.start()
    load_w.start()
    load_feat.start()

    barrier = pltpu.get_barrier_semaphore()
    fixed = [partner] + grp_peers + z_peers
    for peer in fixed:
        pl.semaphore_signal(barrier, inc=1, device_id=peer, device_id_type=pl.DeviceIdType.MESH)
    across = s - 1 + 2 * c
    has_across = jnp.logical_and(across >= 0, across < space)

    @pl.when(has_across)
    def _():
        pl.semaphore_signal(barrier, inc=1, device_id=(g, across), device_id_type=pl.DeviceIdType.MESH)

    row = lax.broadcasted_iota(jnp.int32, (slots, offsets), 0)
    lane = lax.broadcasted_iota(jnp.int32, (1, offsets), 1)
    source = block_map[...]
    local = source - (s * slots - H)
    dead = jnp.logical_and(local - H >= live, local < slots + H)
    skip = jnp.logical_or(jnp.logical_or(source < 0, row >= live), dead)
    place = jnp.where(skip, -1, local)
    tab[...] = jnp.full(tab.shape, empty, jnp.int32)
    tab[0:slots, 0:offsets] = place + base

    def pick(mask):
        found = jnp.max(jnp.where(mask, row, -1), axis=0, keepdims=True)
        return jnp.where(found < 0, empty, found * offsets + lane)

    for a in range(near):
        at = slots + (slots + a if a < H else a - H if a < H + slots else a)
        tab[at : at + 1, 0:offsets] = pick(place == a)
    for b in range(slots):
        same = jnp.logical_and(place == place[b : b + 1, :], row < b)
        tab[slots + near + b : slots + near + b + 1, 0:offsets] = pick(same)
    load_idx = copy(tab, idx, sl.at[3])
    load_idx.start()

    zero = jnp.zeros((height, cin), BF16)
    blocks[empty] = zero
    ext[0] = zero
    edge[2 * H] = zero
    load_top.wait()
    for i in range(H):
        top[i] = top[i] * jnp.where(slots - H + i < live, 1.0, 0.0).astype(BF16)

    def remote(src, dst, send, recv, peer):
        return pltpu.make_async_remote_copy(
            src_ref=src, dst_ref=dst, send_sem=send, recv_sem=recv,
            device_id=peer, device_id_type=pl.DeviceIdType.MESH,
        )

    halo_down = remote(feat.at[pl.ds(0, H)], ext.at[pl.ds(1 + H + slots, H)], sh.at[0], qh.at[0], (g, s - 1))
    halo_up = remote(top, ext.at[pl.ds(1, H)], sh.at[1], qh.at[1], (g, s + 1))
    rim = 2 * slots
    down = remote(fin.at[pl.ds(rim, H)], edge.at[pl.ds(H, H)], sr.at[0], qr.at[0], (g, s - 1))
    up = remote(fin.at[pl.ds(rim + H, H)], edge.at[pl.ds(0, H)], sr.at[1], qr.at[1], (g, s + 1))
    has_down, has_up = s > 0, s < space - 1

    with jax.named_scope("barrier"):
        pl.semaphore_wait(barrier, len(fixed) + has_across.astype(jnp.int32))

    @pl.when(has_down)
    def _():
        halo_down.start()

    @pl.when(has_up)
    def _():
        halo_up.start()

    load_cot.wait()
    load_idx.wait()

    def turn_cot(b, carry):
        turned[b] = cot[b].T
        return carry

    def turn_ext(i, carry):
        blocks[base + i] = ext[1 + i].T
        return carry

    def flip(k, carry):
        w[k] = w[offsets + k].T
        return carry

    part_rows = cot.shape[2] // 2

    def build(b, carry):
        for top_row in range(0, cot.shape[2], part_rows):
            lines = pl.ds(top_row, part_rows)
            mine = turned[b, lines, :]

            def fetch(k):
                return mine + blocks[idx[slots + near + b, k], lines, :]

            ahead = [fetch(k) for k in range(DEPTH)]
            for k in range(offsets):
                if k + DEPTH < offsets:
                    ahead.append(fetch(k + DEPTH))
                blocks[b * offsets + k, lines, :] = ahead[k]
        return carry

    with jax.named_scope("turncot"):
        lax.fori_loop(0, slots, turn_cot, 0, unroll=8)
    load_feat.wait()
    with jax.named_scope("turn"):
        lax.fori_loop(H, H + slots, turn_ext, 0, unroll=8)
    load_w.wait()
    with jax.named_scope("flip"):
        lax.fori_loop(0, offsets, flip, 0, unroll=9 if offsets % 9 == 0 else 1)
    built = slots // 2
    with jax.named_scope("build"):
        lax.fori_loop(0, built, build, 0)

    @pl.when(has_down)
    def _():
        with jax.named_scope("halo1"):
            halo_up.wait_recv()

    @pl.when(jnp.logical_not(has_down))
    def _():
        for i in range(H):
            ext[1 + i] = zero

    @pl.when(has_up)
    def _():
        with jax.named_scope("halo2"):
            halo_down.wait_recv()

    @pl.when(jnp.logical_not(has_up))
    def _():
        for i in range(H):
            ext[1 + H + slots + i] = zero

    parts = slots // WIDE
    chunks = -(-offsets // SPAN)
    direct = rows == padded

    def nth(t):
        return jnp.where(t == 0, 0, jnp.where(t == 1, half - 1, t - 1)) if piped else t

    def weight_chunk(t):
        p = nth(t)
        back = jnp.where(t == 1, chunks * SPAN - offsets, 0) if piped else 0
        start = p * SPAN - back
        rhs = [
            jnp.concatenate([ext[idx[b, start + k] - empty] for b in range(slots)], axis=0)
            for k in range(SPAN)
        ]
        lhs = jnp.concatenate([turned[b] for b in range(slots)], axis=1)
        got = jnp.dot(lhs, jnp.concatenate(rhs, axis=1), preferred_element_type=F32)
        into = part if direct else flat
        for k in range(SPAN):
            to = start + k
            if piped:
                taken = jnp.logical_and(t == chunks - 1, to >= (chunks - 1) * SPAN - (chunks * SPAN - offsets))
                to = jnp.where(taken, offsets + to - (chunks - 1) * SPAN + 1, to)
            at = pl.multiple_of(to * cin, cin)
            into[pl.ds(at, cin), :] = got[:, k * cin : (k + 1) * cin].astype(BF16).T

    def gather_chunk(n):
        kind = jnp.where(n >= parts, offsets, 0)
        lhs = jnp.concatenate([w[kind + k] for k in range(offsets)], axis=1)
        rhs = [
            jnp.concatenate([blocks[idx[n * WIDE + j, k]] for j in range(WIDE)], axis=1)
            for k in range(offsets)
        ]
        got = jnp.dot(lhs, jnp.concatenate(rhs, axis=0), preferred_element_type=F32)
        own = jnp.logical_and(n >= parts, n < 2 * parts)
        for j in range(WIDE):
            i = jnp.where(own, n - parts, n) * WIDE + j
            below = jnp.logical_and(own, i < H)
            above = jnp.logical_and(own, i >= slots - H)
            extra = jnp.where(below, i, jnp.where(above, i - slots + 2 * H, 2 * H))
            factor = jnp.where(jnp.logical_or(n == 2 * parts, i < live), 1.0, 0.0).astype(F32)
            value = got[:, j * height : (j + 1) * height].T + edge[extra].astype(F32)
            fin[n * WIDE + j] = (value * factor).astype(BF16)

    def store(q, near_ref, far_ref, first, sem):
        return copy(near_ref.at[pl.ds(first + q * WIDE, WIDE)], far_ref.at[pl.ds(q * WIDE, WIDE)], sem)

    def piece(p):
        return pl.ds(pl.multiple_of(p * padded, 16), padded)

    here = window_start(g, groups, unit, padded)

    def copy0(i):
        return remote(part.at[piece(2 * i + 1 - c)], r0.at[i], s0.at[i], q0.at[i], partner)

    def copy1(i, d):
        there = window_start((g + d) % groups, groups, unit, padded)
        return remote(
            p1.at[i, pl.ds(there, unit)], r1.at[i, d - 1], s1.at[i, d - 1], q1.at[i, d - 1], grp_peers[d - 1]
        )

    def copy2(i, slot):
        return remote(p2.at[i], r2.at[slot], s2.at[i], q2.at[slot], (g, 2 * i + c))

    def copy3(d):
        return remote(r3.at[0], r3.at[d], s3.at[d - 1], q3.at[d - 1], grp_peers[d - 1])

    def event0(t):
        i = nth(t)
        copy0(i).start()

    def event1(t):
        i = nth(t)
        with jax.named_scope("w0"):
            copy0(i).wait_recv()
        p1[i] = (part[piece(2 * i + c), :].astype(F32) + r0[i].astype(F32)).astype(BF16)
        for d in range(1, groups):
            copy1(i, d).start()

    def event2(t):
        i = nth(t)
        total = p1[i, pl.ds(here, unit), :].astype(F32)
        with jax.named_scope("w1"):
            for d in range(1, groups):
                copy1(i, d).wait_recv()
        for d in range(1, groups):
            total = total + r1[i, d - 1].astype(F32)
        p2[i] = total.astype(BF16)

        @pl.when(z != i)
        def _():
            copy2(i, z).start()

    def event3():
        r2[z] = p2[z]

        def arrive(i, carry):
            @pl.when(z != i)
            def _():
                copy2(i, i).wait_recv()

            return carry

        with jax.named_scope("w2"):
            lax.fori_loop(0, half, arrive, 0)
        total = jnp.zeros((unit, wg.shape[1]), F32)
        for i in range(half):
            total = total + r2[i].astype(F32)
        r3[0] = total.astype(BF16)
        for d in range(1, groups):
            copy3(d).start()

    def span_of(event, first, past):
        lax.fori_loop(first, past, lambda i, carry: (event(i), carry)[1], 0)

    def each(step, lag, event):
        if piped:
            i = step - lag

            @pl.when(jnp.logical_and(i >= 0, i < half))
            def _():
                event(i)

        else:

            @pl.when(step == chunks - 1 + lag)
            def _():
                span_of(event, 0, half)

    steps = chunks + 3 + 2 * parts

    def body(step, carry):
        work = step - chunks - 2

        @pl.when(step < chunks)
        def _():
            with jax.named_scope("wg"):
                weight_chunk(step)

        if not direct:

            @pl.when(step == chunks - 1)
            def _():
                for p in range(space):
                    part[p * padded : p * padded + rows, :] = flat[p * rows : (p + 1) * rows, :]
                    part[p * padded + rows : (p + 1) * padded, :] = jnp.zeros((padded - rows, part.shape[1]), BF16)

        each(step, 0, event0)

        @pl.when(step == chunks)
        def _():
            with jax.named_scope("turn2"):
                lax.fori_loop(0, H, turn_ext, 0, unroll=H)
                lax.fori_loop(H + slots, near, turn_ext, 0, unroll=H)

        @pl.when(step == chunks + 1)
        def _():
            with jax.named_scope("build"):
                lax.fori_loop(built, slots, build, 0)

        @pl.when(work >= 0)
        def _():
            n = jnp.where(work == 0, 2 * parts, work - 1)

            @pl.when(n == parts)
            def _():
                @pl.when(has_down)
                def _():
                    up.wait_recv()

                @pl.when(jnp.logical_not(has_down))
                def _():
                    for i in range(H):
                        edge[i] = zero

                @pl.when(has_up)
                def _():
                    down.wait_recv()

                @pl.when(jnp.logical_not(has_up))
                def _():
                    for i in range(H):
                        edge[H + i] = zero

            with jax.named_scope("gather"):
                gather_chunk(n)

            @pl.when(n < parts)
            def _():
                store(n, fin, out_far, 0, so.at[n]).start()

            @pl.when(jnp.logical_and(n >= parts, n < 2 * parts))
            def _():
                store(n - parts, fin, ig_far, slots, so.at[n]).start()

            @pl.when(n == 2 * parts)
            def _():
                @pl.when(has_down)
                def _():
                    down.start()

                @pl.when(has_up)
                def _():
                    up.start()

        each(step, 1, event1)
        if piped:
            first = step - chunks - 1

            @pl.when(jnp.logical_and(first >= 0, first < half - 1))
            def _():
                span_of(event2, first, jnp.where(first == half - 2, half, first + 1))

        else:

            @pl.when(step == chunks + 2)
            def _():
                span_of(event2, 0, half)

        @pl.when(step == steps - 1 - parts)
        def _():
            event3()

        return carry

    lax.fori_loop(0, steps, body, 0)

    with jax.named_scope("w3"):
        for d in range(1, groups):
            copy3(d).wait_recv()
    for j in range(groups):
        at = min(j * unit, padded - unit)
        wg[at : at + unit, :] = r3[(g - j + groups) % groups].astype(F32)
    store_wg = copy(wg.at[pl.ds(0, rows)], wg_far, so.at[2 * parts])
    store_wg.start()

    with jax.named_scope("drain"):

        @pl.when(has_down)
        def _():
            halo_down.wait_send()
            down.wait_send()

        @pl.when(has_up)
        def _():
            halo_up.wait_send()
            up.wait_send()

        def drain(i, carry):
            copy0(i).wait_send()
            for d in range(1, groups):
                copy1(i, d).wait_send()

            @pl.when(z != i)
            def _():
                copy2(i, z).wait_send()

            return carry

        lax.fori_loop(0, half, drain, 0)
        for d in range(1, groups):
            copy3(d).wait_send()

        def stored(q, carry):
            store(q, fin, out_far, 0, so.at[q]).wait()
            store(q, fin, ig_far, slots, so.at[parts + q]).wait()
            return carry

        lax.fori_loop(0, parts, stored, 0)
        store_wg.wait()


def finish_kernel(out_in, ig_in, wg_in, out_far, ig_far, wg_far, store):
    stores = [
        pltpu.make_async_copy(a, b, store.at[i])
        for i, (a, b) in enumerate([(out_in, out_far), (ig_in, ig_far), (wg_in, wg_far)])
    ]
    for item in stores:
        item.start()
    for item in stores:
        item.wait()


def per_device(features, weights, cotangent, kernel_map, counts):
    voxels = features[0]
    slots, height, cin = voxels.shape
    offsets, _, cout = weights.shape
    space = lax.axis_size("space")
    groups = lax.axis_size("grp")
    near = slots + 2 * H

    half = space // 2
    deep = offsets * cin
    rows = deep // space
    padded = -(-rows // 16) * 16
    unit = -(-padded // (16 * groups)) * 16
    chunks = -(-offsets // SPAN)
    long = chunks * SPAN * cin
    direct = rows == padded
    piped = direct and half == chunks and 2 * rows <= SPAN * cin
    dma = pltpu.SemaphoreType.DMA
    vmem = pltpu.VMEM
    table = 2 * slots + near
    shapes = [((slots, height, cout), BF16), ((slots, height, cin), BF16), ((rows, cout), F32)]

    def stay(x):
        return pltpu.with_memory_space_constraint(x, pltpu.HBM)

    results = pl.pallas_call(
        functools.partial(main_kernel, groups, space, unit, rows, padded, piped),
        out_shape=tuple(vmem(*x) for x in shapes),
        in_specs=[SMEM, VMEM] + [FAR] * 3,
        out_specs=(FAR,) * 3,
        scratch_shapes=[
            vmem((2 * offsets, cin, cout), BF16),
            vmem((slots, height, cout), BF16),
            vmem((slots, cout, height), BF16),
            vmem((slots * offsets + 1 + near, cin, height), BF16),
            vmem((near + 1, height, cin), BF16),
            vmem((H, height, cin), BF16),
            vmem((2 * H + 1, height, cin), BF16),
            vmem((2 * slots + 2 * H, height, cin), BF16),
            vmem((padded, cout), F32),
            vmem((table, 128), jnp.int32),
            pltpu.SMEM((table, 128), jnp.int32),
            vmem((16 if direct else long, cout), BF16),
            vmem((max(long, deep) if direct else space * padded, cout), BF16),
            vmem((half, padded, cout), BF16),
            vmem((half, padded, cout), BF16),
            vmem((half, groups - 1, unit, cout), BF16),
            vmem((half, unit, cout), BF16),
            vmem((half, unit, cout), BF16),
            vmem((groups, unit, cout), BF16),
            dma((5,)),
            dma((2 * (slots // WIDE) + 1,)),
            dma((2,)), dma((2,)),
            dma((2,)), dma((2,)),
            dma((half,)), dma((half,)),
            dma((half, groups - 1)), dma((half, groups - 1)),
            dma((half,)), dma((half,)),
            dma((groups - 1,)), dma((groups - 1,)),
        ],
        compiler_params=pltpu.CompilerParams(
            collective_id=0, has_side_effects=True, vmem_limit_bytes=48 * 1024 * 1024
        ),
        name="main",
    )(counts, kernel_map[0], stay(voxels), stay(weights), stay(cotangent[0]))
    output, input_grad, wg = pl.pallas_call(
        finish_kernel,
        out_shape=tuple(jax.ShapeDtypeStruct(*x) for x in shapes),
        in_specs=[FAR] * 3,
        out_specs=(FAR,) * 3,
        scratch_shapes=[dma((3,))],
        compiler_params=pltpu.CompilerParams(vmem_limit_bytes=4 * 1024 * 1024),
        name="finish",
    )(*results)
    return output[None], input_grad[None], wg


def solution(mesh):
    in_specs = (
        P("grp", "space", None, None),
        P(),
        P("grp", "space", None, None),
        P("grp", "space", None),
        P("grp", "space"),
    )
    out_specs = (P("grp", "space", None, None), P("grp", "space", None, None), P("space", None))
    return jax.shard_map(
        per_device, mesh=mesh, in_specs=in_specs, out_specs=out_specs, check_vma=False
    )
```

time: 40.8 us -> 27.7 us (0.68)
  the two profiles are of different devices: /device:TPU:0 before, /device:TPU:16 now
where the time goes in v1:
time: 27.7 us; the launch traced here: 27.5 us
  Pallas kernels  25.5 us (92%)
  between operations  1.29 us (5%)
  local copies, waits for them, and re-layouts  0.69 us (2%)
    pallas_call x1, Pallas kernels, per_device(): pl.pallas_call(functools.partial(main_kernel, groups, space, unit, rows,...  24.5 us
    pallas_call x1, Pallas kernels, per_device(): pl.pallas_call(finish_kernel, out_shape=tuple((jax.ShapeDtypeStruct(*x) f...  1.06 us
    unnamed x2, local copies, waits for them, and re-layouts  0.69 us

profile of v1, /device:TPU:16, one launch (start us, length us, event | category | flops | bytes accessed | tf_op | source)
XLA Modules:
  0.0 27.5 jit_solution(1446820300366225319)
XLA Ops:
  1.3 0.0 copy-start
  1.3 0.7 %copy-done = s32[1,16,27]{2,1,0:T(8,128)S(1)} copy-done((s32[1,16,27]{2,1,0:T(8,128)S(1)}, s32[1,16,27]{2,1,0:T(8,128)}, u32[]{:S(2)}) %copy-start) | copy-done | bytes 1752
  2.0 24.5 %main.1 = (bf16[16,128,128]{2,1,0:T(8,128)(2,1)S(1)}, bf16[16,128,128]{2,1,0:T(8,128)(2,1)S(1)}, f32[432,128]{1,0:T(8,128)S(1)}) custom-call(s32[1,1]{1,0:T(1,128)S(6)} %copy.8.counts, s32[16,27]{1,0:T(8,128)S(1)} %bitcast.5, bf16[16,128,128]{2,1,0:T(8,128)(2,1)} %bitcast.6, bf16[27,128,128]{2,1,0:T(8,128)(2,1)} %w_far.1, bf16[16,128,128]{2,1,0:T(8,128)(2,1)} %bitcast.7), custom_call_target="tpu_custom_call" | custom-call | tf_op jit(solution)/shard_map/main/pallas_call | solution.py:494
  26.4 1.1 %finish.1 = (bf16[16,128,128]{2,1,0:T(8,128)(2,1)}, bf16[16,128,128]{2,1,0:T(8,128)(2,1)}, f32[432,128]{1,0:T(8,128)}) custom-call(bf16[16,128,128]{2,1,0:T(8,128)(2,1)S(1)} %get-tuple-element.9.out_in, bf16[16,128,128]{2,1,0:T(8,128)(2,1)S(1)} %get-tuple-element.10.ig_in, f32[432,128]{1,0:T(8,128)S(1)} %get-tuple-element.11.wg_in), custom_call_target="tpu_custom_call" | custom-call | tf_op jit(solution)/shard_map/finish/pallas_call | solution.py:533
Async XLA Ops:
  1.3 0.7 %copy-start = (s32[1,16,27]{2,1,0:T(8,128)S(1)}, s32[1,16,27]{2,1,0:T(8,128)}, u32[]{:S(2)}) copy-start(s32[1,16,27]{2,1,0:T(8,128)} %param.8) | copy-start | bytes 5188

commit v2 on v1

--- a/solution.py
+++ b/solution.py
@@ -14,7 +14,6 @@
 BF16, F32 = jnp.bfloat16, jnp.float32
 VMEM = pl.BlockSpec(memory_space=pltpu.VMEM)
 FAR = pl.BlockSpec(memory_space=pl.ANY)
-SMEM = pl.BlockSpec(memory_space=pltpu.SMEM)
 
 
 def window_start(g, groups, unit, rows):
@@ -23,11 +22,11 @@
 
 def main_kernel(
     groups, space, unit, rows, padded, piped,
-    counts, block_map, feat, w_far, cot_far,
+    counts_far, map_far, feat, w_far, cot_far,
     out_far, ig_far, wg_far,
-    w, cot, turned, blocks, ext, top, edge, fin, wg, tab, idx,
+    w, cot, turned, blocks, ext, top, edge, fin, tab, idx, counts, block_map,
     flat, part, r0, p1, r1, p2, r2, r3,
-    sl, so, sh, qh, sr, qr, s0, q0, s1, q1, s2, q2, s3, q3,
+    sl, sh, qh, sr, qr, s0, q0, s1, q1, s2, q2, s3, q3,
 ):
     g = lax.axis_index("grp")
     s = lax.axis_index("space")
@@ -38,20 +37,23 @@
     near = slots + 2 * H
     empty = slots * offsets
     base = empty + 1
-    live = counts[0, 0]
     partner = (g, z * 2 + (1 - c))
     grp_peers = [((g + d) % groups, s) for d in range(1, groups)]
     z_peers = [(g, ((z + d) % half) * 2 + c) for d in range(1, half)]
     copy = pltpu.make_async_copy
 
+    load_counts = copy(counts_far, counts, sl.at[5])
+    load_map = copy(map_far, block_map, sl.at[6])
+    load_counts.start()
+    load_map.start()
     load_top = copy(feat.at[pl.ds(slots - H, H)], top, sl.at[4])
     load_cot = copy(cot_far, cot, sl.at[0])
     load_w = copy(w_far, w.at[pl.ds(offsets, offsets)], sl.at[1])
     load_feat = copy(feat, ext.at[pl.ds(1 + H, slots)], sl.at[2])
     load_top.start()
     load_cot.start()
+    load_feat.start()
     load_w.start()
-    load_feat.start()
 
     barrier = pltpu.get_barrier_semaphore()
     fixed = [partner] + grp_peers + z_peers
@@ -63,6 +65,10 @@
     @pl.when(has_across)
     def _():
         pl.semaphore_signal(barrier, inc=1, device_id=(g, across), device_id_type=pl.DeviceIdType.MESH)
+
+    load_counts.wait()
+    load_map.wait()
+    live = counts[0, 0]
 
     row = lax.broadcasted_iota(jnp.int32, (slots, offsets), 0)
     lane = lax.broadcasted_iota(jnp.int32, (1, offsets), 1)
@@ -78,8 +84,15 @@
         found = jnp.max(jnp.where(mask, row, -1), axis=0, keepdims=True)
         return jnp.where(found < 0, empty, found * offsets + lane)
 
+    def grad_row(a):
+        if H <= a < 2 * H:
+            return slots - 2 * H + a - H
+        if slots <= a < slots + H:
+            return slots - H + a - slots
+        return slots + a if a < H else a - 2 * H if a < slots else a
+
     for a in range(near):
-        at = slots + (slots + a if a < H else a - H if a < H + slots else a)
+        at = slots + grad_row(a)
         tab[at : at + 1, 0:offsets] = pick(place == a)
     for b in range(slots):
         same = jnp.logical_and(place == place[b : b + 1, :], row < b)
@@ -120,7 +133,6 @@
         halo_up.start()
 
     load_cot.wait()
-    load_idx.wait()
 
     def turn_cot(b, carry):
         turned[b] = cot[b].T
@@ -159,7 +171,8 @@
     load_w.wait()
     with jax.named_scope("flip"):
         lax.fori_loop(0, offsets, flip, 0, unroll=9 if offsets % 9 == 0 else 1)
-    built = slots // 2
+    load_idx.wait()
+    built = slots * 5 // 8
     with jax.named_scope("build"):
         lax.fori_loop(0, built, build, 0)
 
@@ -187,13 +200,8 @@
     chunks = -(-offsets // SPAN)
     direct = rows == padded
 
-    def nth(t):
-        return jnp.where(t == 0, 0, jnp.where(t == 1, half - 1, t - 1)) if piped else t
-
     def weight_chunk(t):
-        p = nth(t)
-        back = jnp.where(t == 1, chunks * SPAN - offsets, 0) if piped else 0
-        start = p * SPAN - back
+        start = t * SPAN
         rhs = [
             jnp.concatenate([ext[idx[b, start + k] - empty] for b in range(slots)], axis=0)
             for k in range(SPAN)
@@ -202,11 +210,7 @@
         got = jnp.dot(lhs, jnp.concatenate(rhs, axis=1), preferred_element_type=F32)
         into = part if direct else flat
         for k in range(SPAN):
-            to = start + k
-            if piped:
-                taken = jnp.logical_and(t == chunks - 1, to >= (chunks - 1) * SPAN - (chunks * SPAN - offsets))
-                to = jnp.where(taken, offsets + to - (chunks - 1) * SPAN + 1, to)
-            at = pl.multiple_of(to * cin, cin)
+            at = pl.multiple_of((start + k) * cin, cin)
             into[pl.ds(at, cin), :] = got[:, k * cin : (k + 1) * cin].astype(BF16).T
 
     def gather_chunk(n):
@@ -217,18 +221,24 @@
             for k in range(offsets)
         ]
         got = jnp.dot(lhs, jnp.concatenate(rhs, axis=0), preferred_element_type=F32)
-        own = jnp.logical_and(n >= parts, n < 2 * parts)
+        outer = n == 2 * parts - 1
         for j in range(WIDE):
-            i = jnp.where(own, n - parts, n) * WIDE + j
-            below = jnp.logical_and(own, i < H)
-            above = jnp.logical_and(own, i >= slots - H)
-            extra = jnp.where(below, i, jnp.where(above, i - slots + 2 * H, 2 * H))
+            i = jnp.where(n < parts, n, n - parts) * WIDE + j
+            i = jnp.where(n < parts, i, jnp.where(outer, j if j < H else slots - WIDE + j, i + H))
+            extra = jnp.where(outer, j, 2 * H)
             factor = jnp.where(jnp.logical_or(n == 2 * parts, i < live), 1.0, 0.0).astype(F32)
             value = got[:, j * height : (j + 1) * height].T + edge[extra].astype(F32)
             fin[n * WIDE + j] = (value * factor).astype(BF16)
 
-    def store(q, near_ref, far_ref, first, sem):
-        return copy(near_ref.at[pl.ds(first + q * WIDE, WIDE)], far_ref.at[pl.ds(q * WIDE, WIDE)], sem)
+    def store_out(q):
+        return copy(fin.at[pl.ds(q * WIDE, WIDE)], out_far.at[pl.ds(q * WIDE, WIDE)], sl.at[q])
+
+    def store_inner(q):
+        return copy(fin.at[pl.ds(slots + q * WIDE, WIDE)], ig_far.at[pl.ds(H + q * WIDE, WIDE)], sl.at[parts + q])
+
+    def store_outer(side):
+        at = 2 * slots - WIDE + side * H
+        return copy(fin.at[pl.ds(at, H)], ig_far.at[pl.ds(side * (slots - H), H)], sl.at[2 * parts - 1 + side])
 
     def piece(p):
         return pl.ds(pl.multiple_of(p * padded, 16), padded)
@@ -236,38 +246,37 @@
     here = window_start(g, groups, unit, padded)
 
     def copy0(i):
-        return remote(part.at[piece(2 * i + 1 - c)], r0.at[i], s0.at[i], q0.at[i], partner)
+        return remote(part.at[piece(2 * i + 1 - c)], r0.at[i], s0, q0.at[i], partner)
 
     def copy1(i, d):
         there = window_start((g + d) % groups, groups, unit, padded)
         return remote(
-            p1.at[i, pl.ds(there, unit)], r1.at[i, d - 1], s1.at[i, d - 1], q1.at[i, d - 1], grp_peers[d - 1]
+            p1.at[i, pl.ds(there, unit)], r1.at[i, d - 1], s1, q1.at[i], grp_peers[d - 1]
         )
 
     def copy2(i, slot):
-        return remote(p2.at[i], r2.at[slot], s2.at[i], q2.at[slot], (g, 2 * i + c))
+        return remote(p2.at[i], r2.at[slot], s2, q2, (g, 2 * i + c))
+
+    def wait(like, sem):
+        copy(like, like, sem).wait()
 
     def copy3(d):
-        return remote(r3.at[0], r3.at[d], s3.at[d - 1], q3.at[d - 1], grp_peers[d - 1])
-
-    def event0(t):
-        i = nth(t)
+        return remote(r3.at[0], r3.at[d], s3, q3, grp_peers[d - 1])
+
+    def event0(i):
         copy0(i).start()
 
-    def event1(t):
-        i = nth(t)
+    def event1(i):
         with jax.named_scope("w0"):
             copy0(i).wait_recv()
         p1[i] = (part[piece(2 * i + c), :].astype(F32) + r0[i].astype(F32)).astype(BF16)
         for d in range(1, groups):
             copy1(i, d).start()
 
-    def event2(t):
-        i = nth(t)
+    def event2(i):
         total = p1[i, pl.ds(here, unit), :].astype(F32)
         with jax.named_scope("w1"):
-            for d in range(1, groups):
-                copy1(i, d).wait_recv()
+            wait(r1.at[i], q1.at[i])
         for d in range(1, groups):
             total = total + r1[i, d - 1].astype(F32)
         p2[i] = total.astype(BF16)
@@ -277,18 +286,10 @@
             copy2(i, z).start()
 
     def event3():
+        with jax.named_scope("w2"):
+            wait(r2.at[pl.ds(0, half - 1)], q2)
         r2[z] = p2[z]
-
-        def arrive(i, carry):
-            @pl.when(z != i)
-            def _():
-                copy2(i, i).wait_recv()
-
-            return carry
-
-        with jax.named_scope("w2"):
-            lax.fori_loop(0, half, arrive, 0)
-        total = jnp.zeros((unit, wg.shape[1]), F32)
+        total = jnp.zeros((unit, cot.shape[2]), F32)
         for i in range(half):
             total = total + r2[i].astype(F32)
         r3[0] = total.astype(BF16)
@@ -347,7 +348,7 @@
         def _():
             n = jnp.where(work == 0, 2 * parts, work - 1)
 
-            @pl.when(n == parts)
+            @pl.when(n == 2 * parts - 1)
             def _():
                 @pl.when(has_down)
                 def _():
@@ -372,21 +373,16 @@
 
             @pl.when(n < parts)
             def _():
-                store(n, fin, out_far, 0, so.at[n]).start()
-
-            @pl.when(jnp.logical_and(n >= parts, n < 2 * parts))
-            def _():
-                store(n - parts, fin, ig_far, slots, so.at[n]).start()
-
-            @pl.when(n == 2 * parts)
-            def _():
-                @pl.when(has_down)
-                def _():
-                    down.start()
-
-                @pl.when(has_up)
-                def _():
-                    up.start()
+                store_out(n).start()
+
+            @pl.when(jnp.logical_and(n >= parts, n < 2 * parts - 1))
+            def _():
+                store_inner(n - parts).start()
+
+            @pl.when(n == 2 * parts - 1)
+            def _():
+                store_outer(0).start()
+                store_outer(1).start()
 
         each(step, 1, event1)
         if piped:
@@ -402,7 +398,17 @@
             def _():
                 span_of(event2, 0, half)
 
-        @pl.when(step == steps - 1 - parts)
+        @pl.when(work == 0)
+        def _():
+            @pl.when(has_down)
+            def _():
+                down.start()
+
+            @pl.when(has_up)
+            def _():
+                up.start()
+
+        @pl.when(step == (steps - 3 + (z + 1) // 2 if piped else steps - 1))
         def _():
             event3()
 
@@ -411,13 +417,11 @@
     lax.fori_loop(0, steps, body, 0)
 
     with jax.named_scope("w3"):
-        for d in range(1, groups):
-            copy3(d).wait_recv()
+        wait(r3.at[pl.ds(1, groups - 1)], q3)
     for j in range(groups):
         at = min(j * unit, padded - unit)
-        wg[at : at + unit, :] = r3[(g - j + groups) % groups].astype(F32)
-    store_wg = copy(wg.at[pl.ds(0, rows)], wg_far, so.at[2 * parts])
-    store_wg.start()
+        length = min(unit, rows - at)
+        wg_far[at : at + length, :] = r3[(g - j + groups) % groups, 0:length, :].astype(F32)
 
     with jax.named_scope("drain"):
 
@@ -431,28 +435,23 @@
             halo_up.wait_send()
             up.wait_send()
 
-        def drain(i, carry):
-            copy0(i).wait_send()
-            for d in range(1, groups):
-                copy1(i, d).wait_send()
-
-            @pl.when(z != i)
-            def _():
-                copy2(i, z).wait_send()
-
+        wait(r0, s0)
+        wait(r1, s1)
+        wait(r2.at[pl.ds(0, half - 1)], s2)
+        wait(r3.at[pl.ds(1, groups - 1)], s3)
+
+        def stored(q, carry):
+            store_out(q).wait()
             return carry
 
-        lax.fori_loop(0, half, drain, 0)
-        for d in range(1, groups):
-            copy3(d).wait_send()
-
-        def stored(q, carry):
-            store(q, fin, out_far, 0, so.at[q]).wait()
-            store(q, fin, ig_far, slots, so.at[parts + q]).wait()
+        def stored_inner(q, carry):
+            store_inner(q).wait()
             return carry
 
         lax.fori_loop(0, parts, stored, 0)
-        store_wg.wait()
+        lax.fori_loop(0, parts - 1, stored_inner, 0)
+        store_outer(0).wait()
+        store_outer(1).wait()
 
 
 def finish_kernel(out_in, ig_in, wg_in, out_far, ig_far, wg_far, store):
@@ -494,8 +493,8 @@
     results = pl.pallas_call(
         functools.partial(main_kernel, groups, space, unit, rows, padded, piped),
         out_shape=tuple(vmem(*x) for x in shapes),
-        in_specs=[SMEM, VMEM] + [FAR] * 3,
-        out_specs=(FAR,) * 3,
+        in_specs=[FAR] * 5,
+        out_specs=(FAR, FAR, VMEM),
         scratch_shapes=[
             vmem((2 * offsets, cin, cout), BF16),
             vmem((slots, height, cout), BF16),
@@ -505,9 +504,10 @@
             vmem((H, height, cin), BF16),
             vmem((2 * H + 1, height, cin), BF16),
             vmem((2 * slots + 2 * H, height, cin), BF16),
-            vmem((padded, cout), F32),
             vmem((table, 128), jnp.int32),
             pltpu.SMEM((table, 128), jnp.int32),
+            pltpu.SMEM((1, 1), jnp.int32),
+            vmem((slots, offsets), jnp.int32),
             vmem((16 if direct else long, cout), BF16),
             vmem((max(long, deep) if direct else space * padded, cout), BF16),
             vmem((half, padded, cout), BF16),
@@ -516,20 +516,19 @@
             vmem((half, unit, cout), BF16),
             vmem((half, unit, cout), BF16),
             vmem((groups, unit, cout), BF16),
-            dma((5,)),
-            dma((2 * (slots // WIDE) + 1,)),
+            dma((max(7, 2 * (slots // WIDE) + 2),)),
             dma((2,)), dma((2,)),
             dma((2,)), dma((2,)),
-            dma((half,)), dma((half,)),
-            dma((half, groups - 1)), dma((half, groups - 1)),
-            dma((half,)), dma((half,)),
-            dma((groups - 1,)), dma((groups - 1,)),
+            dma, dma((half,)),
+            dma, dma((half,)),
+            dma, dma,
+            dma, dma,
         ],
         compiler_params=pltpu.CompilerParams(
             collective_id=0, has_side_effects=True, vmem_limit_bytes=48 * 1024 * 1024
         ),
         name="main",
-    )(counts, kernel_map[0], stay(voxels), stay(weights), stay(cotangent[0]))
+    )(counts, stay(kernel_map[0]), stay(voxels), stay(weights), stay(cotangent[0]))
     output, input_grad, wg = pl.pallas_call(
         finish_kernel,
         out_shape=tuple(jax.ShapeDtypeStruct(*x) for x in shapes),

time: 27.7 us -> 26.1 us (0.942)
  the two profiles are of different devices: /device:TPU:16 before, /device:TPU:0 now
where the time goes in v2:
time: 26.1 us; the launch traced here: 25.9 us
  Pallas kernels  24.6 us (94%)
  between operations  1.29 us (5%)
    pallas_call x1, Pallas kernels, per_device(): pl.pallas_call(functools.partial(main_kernel, groups, space, unit, rows,...  23.5 us
    pallas_call x1, Pallas kernels, per_device(): pl.pallas_call(finish_kernel, out_shape=tuple((jax.ShapeDtypeStruct(*x) f...  1.06 us

profile of v2, /device:TPU:0, one launch (start us, length us, event | category | flops | bytes accessed | tf_op | source)
XLA Modules:
  0.0 25.9 jit_solution(7211238848239988472)
XLA Ops:
  1.3 23.5 %main.1 = (bf16[16,128,128]{2,1,0:T(8,128)(2,1)S(1)}, bf16[16,128,128]{2,1,0:T(8,128)(2,1)S(1)}, f32[432,128]{1,0:T(8,128)S(1)}) custom-call(s32[1,1]{1,0:T(1,128)S(6)} %copy.8.counts_far, s32[16,27]{1,0:T(8,128)} %bitcast.7, bf16[16,128,128]{2,1,0:T(8,128)(2,1)} %bitcast.5, bf16[27,128,128]{2,1,0:T(8,128)(2,1)} %w_far.1, bf16[16,128,128]{2,1,0:T(8,128)(2,1)} %bitcast.6), custom_call_target="tpu_custom_call" | custom-call | tf_op jit(solution)/shard_map/main/pallas_call | solution.py:493
  24.8 1.1 %finish.1 = (bf16[16,128,128]{2,1,0:T(8,128)(2,1)}, bf16[16,128,128]{2,1,0:T(8,128)(2,1)}, f32[432,128]{1,0:T(8,128)}) custom-call(bf16[16,128,128]{2,1,0:T(8,128)(2,1)S(1)} %get-tuple-element.9.out_in, bf16[16,128,128]{2,1,0:T(8,128)(2,1)S(1)} %get-tuple-element.10.ig_in, f32[432,128]{1,0:T(8,128)S(1)} %get-tuple-element.11.wg_in), custom_call_target="tpu_custom_call" | custom-call | tf_op jit(solution)/shard_map/finish/pallas_call | solution.py:532

commit v3 on v2

--- a/solution.py
+++ b/solution.py
@@ -10,7 +10,7 @@
 H = 4
 WIDE = 2 * H
 SPAN = 7
-DEPTH = 4
+BUILT, PAUSED = 11, 13
 BF16, F32 = jnp.bfloat16, jnp.float32
 VMEM = pl.BlockSpec(memory_space=pltpu.VMEM)
 FAR = pl.BlockSpec(memory_space=pl.ANY)
@@ -23,8 +23,8 @@
 def main_kernel(
     groups, space, unit, rows, padded, piped,
     counts_far, map_far, feat, w_far, cot_far,
-    out_far, ig_far, wg_far,
-    w, cot, turned, blocks, ext, top, edge, fin, tab, idx, counts, block_map,
+    fin, wg_far,
+    w, cot, turned, blocks, ext, top, edge, tab, idx, counts, block_map,
     flat, part, r0, p1, r1, p2, r2, r3,
     sl, sh, qh, sr, qr, s0, q0, s1, q1, s2, q2, s3, q3,
 ):
@@ -41,6 +41,19 @@
     grp_peers = [((g + d) % groups, s) for d in range(1, groups)]
     z_peers = [(g, ((z + d) % half) * 2 + c) for d in range(1, half)]
     copy = pltpu.make_async_copy
+    far = 3 - 2 * (g % 2)
+    turns = [far, 2, 4 - far] if groups == 4 else list(range(1, groups))
+
+    barrier = pltpu.get_barrier_semaphore()
+    fixed = [partner] + grp_peers + z_peers
+    for peer in fixed:
+        pl.semaphore_signal(barrier, inc=1, device_id=peer, device_id_type=pl.DeviceIdType.MESH)
+    across = s - 1 + 2 * c
+    has_across = jnp.logical_and(across >= 0, across < space)
+
+    @pl.when(has_across)
+    def _():
+        pl.semaphore_signal(barrier, inc=1, device_id=(g, across), device_id_type=pl.DeviceIdType.MESH)
 
     load_counts = copy(counts_far, counts, sl.at[5])
     load_map = copy(map_far, block_map, sl.at[6])
@@ -55,20 +68,41 @@
     load_feat.start()
     load_w.start()
 
-    barrier = pltpu.get_barrier_semaphore()
-    fixed = [partner] + grp_peers + z_peers
-    for peer in fixed:
-        pl.semaphore_signal(barrier, inc=1, device_id=peer, device_id_type=pl.DeviceIdType.MESH)
-    across = s - 1 + 2 * c
-    has_across = jnp.logical_and(across >= 0, across < space)
-
-    @pl.when(has_across)
-    def _():
-        pl.semaphore_signal(barrier, inc=1, device_id=(g, across), device_id_type=pl.DeviceIdType.MESH)
+    zero = jnp.zeros((height, cin), BF16)
+    blocks[empty] = zero
+    ext[0] = zero
+    edge[2 * H] = zero
+    def remote(src, dst, send, recv, peer):
+        return pltpu.make_async_remote_copy(
+            src_ref=src, dst_ref=dst, send_sem=send, recv_sem=recv,
+            device_id=peer, device_id_type=pl.DeviceIdType.MESH,
+        )
+
+    halo_down = remote(feat.at[pl.ds(0, H)], ext.at[pl.ds(1 + H + slots, H)], sh.at[0], qh.at[0], (g, s - 1))
+    halo_up = remote(top, ext.at[pl.ds(1, H)], sh.at[1], qh.at[1], (g, s + 1))
+    rim = 2 * slots
+    down = remote(fin.at[pl.ds(rim, H)], edge.at[pl.ds(H, H)], sr.at[0], qr.at[0], (g, s - 1))
+    up = remote(fin.at[pl.ds(rim + H, H)], edge.at[pl.ds(0, H)], sr.at[1], qr.at[1], (g, s + 1))
+    has_down, has_up = s > 0, s < space - 1
+
+    with jax.named_scope("barrier"):
+        pl.semaphore_wait(barrier, len(fixed) + has_across.astype(jnp.int32))
+
+    @pl.when(has_down)
+    def _():
+        halo_down.start()
 
     load_counts.wait()
+    live = counts[0, 0]
+    load_top.wait()
+    for i in range(H):
+        top[i] = top[i] * jnp.where(slots - H + i < live, 1.0, 0.0).astype(BF16)
+
+    @pl.when(has_up)
+    def _():
+        halo_up.start()
+
     load_map.wait()
-    live = counts[0, 0]
 
     row = lax.broadcasted_iota(jnp.int32, (slots, offsets), 0)
     lane = lax.broadcasted_iota(jnp.int32, (1, offsets), 1)
@@ -100,38 +134,6 @@
     load_idx = copy(tab, idx, sl.at[3])
     load_idx.start()
 
-    zero = jnp.zeros((height, cin), BF16)
-    blocks[empty] = zero
-    ext[0] = zero
-    edge[2 * H] = zero
-    load_top.wait()
-    for i in range(H):
-        top[i] = top[i] * jnp.where(slots - H + i < live, 1.0, 0.0).astype(BF16)
-
-    def remote(src, dst, send, recv, peer):
-        return pltpu.make_async_remote_copy(
-            src_ref=src, dst_ref=dst, send_sem=send, recv_sem=recv,
-            device_id=peer, device_id_type=pl.DeviceIdType.MESH,
-        )
-
-    halo_down = remote(feat.at[pl.ds(0, H)], ext.at[pl.ds(1 + H + slots, H)], sh.at[0], qh.at[0], (g, s - 1))
-    halo_up = remote(top, ext.at[pl.ds(1, H)], sh.at[1], qh.at[1], (g, s + 1))
-    rim = 2 * slots
-    down = remote(fin.at[pl.ds(rim, H)], edge.at[pl.ds(H, H)], sr.at[0], qr.at[0], (g, s - 1))
-    up = remote(fin.at[pl.ds(rim + H, H)], edge.at[pl.ds(0, H)], sr.at[1], qr.at[1], (g, s + 1))
-    has_down, has_up = s > 0, s < space - 1
-
-    with jax.named_scope("barrier"):
-        pl.semaphore_wait(barrier, len(fixed) + has_across.astype(jnp.int32))
-
-    @pl.when(has_down)
-    def _():
-        halo_down.start()
-
-    @pl.when(has_up)
-    def _():
-        halo_up.start()
-
     load_cot.wait()
 
     def turn_cot(b, carry):
@@ -146,21 +148,17 @@
         w[k] = w[offsets + k].T
         return carry
 
-    part_rows = cot.shape[2] // 2
-
     def build(b, carry):
-        for top_row in range(0, cot.shape[2], part_rows):
-            lines = pl.ds(top_row, part_rows)
-            mine = turned[b, lines, :]
-
-            def fetch(k):
-                return mine + blocks[idx[slots + near + b, k], lines, :]
-
-            ahead = [fetch(k) for k in range(DEPTH)]
-            for k in range(offsets):
-                if k + DEPTH < offsets:
-                    ahead.append(fetch(k + DEPTH))
-                blocks[b * offsets + k, lines, :] = ahead[k]
+        mine = turned[b]
+
+        def fetch(k):
+            return mine + blocks[idx[slots + near + b, k]]
+
+        ahead = fetch(0)
+        for k in range(offsets):
+            following = fetch(k + 1) if k + 1 < offsets else None
+            blocks[b * offsets + k] = ahead
+            ahead = following
         return carry
 
     with jax.named_scope("turncot"):
@@ -172,7 +170,7 @@
     with jax.named_scope("flip"):
         lax.fori_loop(0, offsets, flip, 0, unroll=9 if offsets % 9 == 0 else 1)
     load_idx.wait()
-    built = slots * 5 // 8
+    built, paused = slots * BUILT // 16, slots * PAUSED // 16
     with jax.named_scope("build"):
         lax.fori_loop(0, built, build, 0)
 
@@ -200,8 +198,12 @@
     chunks = -(-offsets // SPAN)
     direct = rows == padded
 
+    def nth(t):
+        return jnp.where(t == 0, 0, jnp.where(t == 1, half - 1, t - 1)) if piped else t
+
     def weight_chunk(t):
-        start = t * SPAN
+        spare = chunks * SPAN - offsets
+        start = nth(t) * SPAN - (jnp.where(t == 1, spare, 0) if piped else 0)
         rhs = [
             jnp.concatenate([ext[idx[b, start + k] - empty] for b in range(slots)], axis=0)
             for k in range(SPAN)
@@ -210,7 +212,10 @@
         got = jnp.dot(lhs, jnp.concatenate(rhs, axis=1), preferred_element_type=F32)
         into = part if direct else flat
         for k in range(SPAN):
-            at = pl.multiple_of((start + k) * cin, cin)
+            to = start + k
+            if piped and k >= SPAN - spare:
+                to = jnp.where(t == chunks - 1, (chunks - 1) * SPAN + k, to)
+            at = pl.multiple_of(to * cin, cin)
             into[pl.ds(at, cin), :] = got[:, k * cin : (k + 1) * cin].astype(BF16).T
 
     def gather_chunk(n):
@@ -230,16 +235,6 @@
             value = got[:, j * height : (j + 1) * height].T + edge[extra].astype(F32)
             fin[n * WIDE + j] = (value * factor).astype(BF16)
 
-    def store_out(q):
-        return copy(fin.at[pl.ds(q * WIDE, WIDE)], out_far.at[pl.ds(q * WIDE, WIDE)], sl.at[q])
-
-    def store_inner(q):
-        return copy(fin.at[pl.ds(slots + q * WIDE, WIDE)], ig_far.at[pl.ds(H + q * WIDE, WIDE)], sl.at[parts + q])
-
-    def store_outer(side):
-        at = 2 * slots - WIDE + side * H
-        return copy(fin.at[pl.ds(at, H)], ig_far.at[pl.ds(side * (slots - H), H)], sl.at[2 * parts - 1 + side])
-
     def piece(p):
         return pl.ds(pl.multiple_of(p * padded, 16), padded)
 
@@ -251,7 +246,7 @@
     def copy1(i, d):
         there = window_start((g + d) % groups, groups, unit, padded)
         return remote(
-            p1.at[i, pl.ds(there, unit)], r1.at[i, d - 1], s1, q1.at[i], grp_peers[d - 1]
+            p1.at[i, pl.ds(there, unit)], r1.at[i, d - 1], s1, q1.at[i], ((g + d) % groups, s)
         )
 
     def copy2(i, slot):
@@ -261,19 +256,22 @@
         copy(like, like, sem).wait()
 
     def copy3(d):
-        return remote(r3.at[0], r3.at[d], s3, q3, grp_peers[d - 1])
-
-    def event0(i):
+        return remote(r3.at[0], r3.at[d], s3, q3, ((g + d) % groups, s))
+
+    def event0(t):
+        i = nth(t)
         copy0(i).start()
 
-    def event1(i):
+    def event1(t):
+        i = nth(t)
         with jax.named_scope("w0"):
             copy0(i).wait_recv()
         p1[i] = (part[piece(2 * i + c), :].astype(F32) + r0[i].astype(F32)).astype(BF16)
-        for d in range(1, groups):
+        for d in turns:
             copy1(i, d).start()
 
-    def event2(i):
+    def event2(t):
+        i = nth(t)
         total = p1[i, pl.ds(here, unit), :].astype(F32)
         with jax.named_scope("w1"):
             wait(r1.at[i], q1.at[i])
@@ -293,7 +291,7 @@
         for i in range(half):
             total = total + r2[i].astype(F32)
         r3[0] = total.astype(BF16)
-        for d in range(1, groups):
+        for d in turns:
             copy3(d).start()
 
     def span_of(event, first, past):
@@ -339,10 +337,11 @@
                 lax.fori_loop(0, H, turn_ext, 0, unroll=H)
                 lax.fori_loop(H + slots, near, turn_ext, 0, unroll=H)
 
-        @pl.when(step == chunks + 1)
+        @pl.when(jnp.logical_and(step >= chunks, work < 0))
         def _():
             with jax.named_scope("build"):
-                lax.fori_loop(built, slots, build, 0)
+                first = jnp.where(step == chunks, built, paused)
+                lax.fori_loop(first, jnp.where(step == chunks, paused, slots), build, 0)
 
         @pl.when(work >= 0)
         def _():
@@ -371,19 +370,6 @@
             with jax.named_scope("gather"):
                 gather_chunk(n)
 
-            @pl.when(n < parts)
-            def _():
-                store_out(n).start()
-
-            @pl.when(jnp.logical_and(n >= parts, n < 2 * parts - 1))
-            def _():
-                store_inner(n - parts).start()
-
-            @pl.when(n == 2 * parts - 1)
-            def _():
-                store_outer(0).start()
-                store_outer(1).start()
-
         each(step, 1, event1)
         if piped:
             first = step - chunks - 1
@@ -408,7 +394,7 @@
             def _():
                 up.start()
 
-        @pl.when(step == (steps - 3 + (z + 1) // 2 if piped else steps - 1))
+        @pl.when(step == (steps - 4 + 2 * jnp.minimum(z, 1) if piped else steps - 1))
         def _():
             event3()
 
@@ -440,25 +426,18 @@
         wait(r2.at[pl.ds(0, half - 1)], s2)
         wait(r3.at[pl.ds(1, groups - 1)], s3)
 
-        def stored(q, carry):
-            store_out(q).wait()
-            return carry
-
-        def stored_inner(q, carry):
-            store_inner(q).wait()
-            return carry
-
-        lax.fori_loop(0, parts, stored, 0)
-        lax.fori_loop(0, parts - 1, stored_inner, 0)
-        store_outer(0).wait()
-        store_outer(1).wait()
-
-
-def finish_kernel(out_in, ig_in, wg_in, out_far, ig_far, wg_far, store):
-    stores = [
-        pltpu.make_async_copy(a, b, store.at[i])
-        for i, (a, b) in enumerate([(out_in, out_far), (ig_in, ig_far), (wg_in, wg_far)])
+
+def finish_kernel(fin, wg_in, out_far, ig_far, wg_far, store):
+    slots = out_far.shape[0]
+    inner = slots - 2 * H
+    moves = [
+        (fin.at[pl.ds(0, slots)], out_far),
+        (fin.at[pl.ds(slots, inner)], ig_far.at[pl.ds(H, inner)]),
+        (fin.at[pl.ds(slots + inner, H)], ig_far.at[pl.ds(0, H)]),
+        (fin.at[pl.ds(2 * slots - H, H)], ig_far.at[pl.ds(slots - H, H)]),
+        (wg_in, wg_far),
     ]
+    stores = [pltpu.make_async_copy(a, b, store.at[i]) for i, (a, b) in enumerate(moves)]
     for item in stores:
         item.start()
     for item in stores:
@@ -492,9 +471,9 @@
 
     results = pl.pallas_call(
         functools.partial(main_kernel, groups, space, unit, rows, padded, piped),
-        out_shape=tuple(vmem(*x) for x in shapes),
+        out_shape=(vmem((2 * slots + 2 * H, height, cout), BF16), vmem(*shapes[2])),
         in_specs=[FAR] * 5,
-        out_specs=(FAR, FAR, VMEM),
+        out_specs=(VMEM, VMEM),
         scratch_shapes=[
             vmem((2 * offsets, cin, cout), BF16),
             vmem((slots, height, cout), BF16),
@@ -503,7 +482,6 @@
             vmem((near + 1, height, cin), BF16),
             vmem((H, height, cin), BF16),
             vmem((2 * H + 1, height, cin), BF16),
-            vmem((2 * slots + 2 * H, height, cin), BF16),
             vmem((table, 128), jnp.int32),
             pltpu.SMEM((table, 128), jnp.int32),
             pltpu.SMEM((1, 1), jnp.int32),
@@ -516,7 +494,7 @@
             vmem((half, unit, cout), BF16),
             vmem((half, unit, cout), BF16),
             vmem((groups, unit, cout), BF16),
-            dma((max(7, 2 * (slots // WIDE) + 2),)),
+            dma((7,)),
             dma((2,)), dma((2,)),
             dma((2,)), dma((2,)),
             dma, dma((half,)),
@@ -532,9 +510,9 @@
     output, input_grad, wg = pl.pallas_call(
         finish_kernel,
         out_shape=tuple(jax.ShapeDtypeStruct(*x) for x in shapes),
-        in_specs=[FAR] * 3,
+        in_specs=[FAR] * 2,
         out_specs=(FAR,) * 3,
-        scratch_shapes=[dma((3,))],
+        scratch_shapes=[dma((5,))],
         compiler_params=pltpu.CompilerParams(vmem_limit_bytes=4 * 1024 * 1024),
         name="finish",
     )(*results)

time: 26.1 us -> 25.6 us (0.981)
  the two profiles are of different devices: /device:TPU:0 before, /device:TPU:16 now
where the time goes in v3:
time: 25.6 us; the launch traced here: 25.1 us
  Pallas kernels  23.9 us (93%)
  between operations  1.29 us (5%)
    pallas_call x1, Pallas kernels, per_device(): pl.pallas_call(functools.partial(main_kernel, groups, space, unit, rows,...  22.8 us
    pallas_call x1, Pallas kernels, per_device(): pl.pallas_call(finish_kernel, out_shape=tuple((jax.ShapeDtypeStruct(*x) f...  1.08 us

profile of v3, /device:TPU:16, one launch (start us, length us, event | category | flops | bytes accessed | tf_op | source)
XLA Modules:
  0.0 25.1 jit_solution(12058311213315583601)
XLA Ops:
  1.3 22.8 %main.1 = (bf16[40,128,128]{2,1,0:T(8,128)(2,1)S(1)}, f32[432,128]{1,0:T(8,128)S(1)}) custom-call(s32[1,1]{1,0:T(1,128)S(6)} %copy.8.counts_far, s32[16,27]{1,0:T(8,128)} %bitcast.7, bf16[16,128,128]{2,1,0:T(8,128)(2,1)} %bitcast.5, bf16[27,128,128]{2,1,0:T(8,128)(2,1)} %w_far.1, bf16[16,128,128]{2,1,0:T(8,128)(2,1)} %bitcast.6), custom_call_target="tpu_custom_call" | custom-call | tf_op jit(solution)/shard_map/main/pallas_call | solution.py:472
  24.1 1.1 %finish.1 = (bf16[16,128,128]{2,1,0:T(8,128)(2,1)}, bf16[16,128,128]{2,1,0:T(8,128)(2,1)}, f32[432,128]{1,0:T(8,128)}) custom-call(bf16[40,128,128]{2,1,0:T(8,128)(2,1)S(1)} %get-tuple-element.8.fin, f32[432,128]{1,0:T(8,128)S(1)} %get-tuple-element.9.wg_in), custom_call_target="tpu_custom_call" | custom-call | tf_op jit(solution)/shard_map/finish/pallas_call | solution.py:510

commit v4 on v3

--- a/solution.py
+++ b/solution.py
@@ -313,6 +313,15 @@
 
     steps = chunks + 3 + 2 * parts
 
+    early = jnp.where(jnp.logical_and(z == 0, g == 0), 1, 0)
+
+    def ready(step):
+        counts_at = [jnp.minimum(z, 1), 2, half - early]
+        number = jnp.where(step > chunks, half, 0)
+        for j, value in enumerate(counts_at):
+            number = jnp.where(step == chunks + 1 + j, value, number)
+        return number
+
     def body(step, carry):
         work = step - chunks - 2
 
@@ -372,11 +381,7 @@
 
         each(step, 1, event1)
         if piped:
-            first = step - chunks - 1
-
-            @pl.when(jnp.logical_and(first >= 0, first < half - 1))
-            def _():
-                span_of(event2, first, jnp.where(first == half - 2, half, first + 1))
+            span_of(event2, ready(step - 1), ready(step))
 
         else:
 
@@ -384,17 +389,15 @@
             def _():
                 span_of(event2, 0, half)
 
-        @pl.when(work == 0)
-        def _():
-            @pl.when(has_down)
-            def _():
-                down.start()
-
-            @pl.when(has_up)
-            def _():
-                up.start()
-
-        @pl.when(step == (steps - 4 + 2 * jnp.minimum(z, 1) if piped else steps - 1))
+        @pl.when(jnp.logical_and(work == jnp.where(z > 1, 1 - c, 0), has_down))
+        def _():
+            down.start()
+
+        @pl.when(jnp.logical_and(work == 2 * c, has_up))
+        def _():
+            up.start()
+
+        @pl.when(step == (steps - 4 + 2 * jnp.minimum(z, 1) + early if piped else steps - 1))
         def _():
             event3()
 

time: 25.6 us -> 25.1 us (0.980)
  Pallas kernels: 23.9 us -> 23.6 us
    pallas_call x1, Pallas kernels: 22.8 us -> 22.5 us  [per_device(): pl.pallas_call(functools.partial(main_kernel, groups, space, unit, rows,...]
where the time goes in v4:
time: 25.1 us; the launch traced here: 24.9 us
  Pallas kernels  23.6 us (94%)
  between operations  1.29 us (5%)
    pallas_call x1, Pallas kernels, per_device(): pl.pallas_call(functools.partial(main_kernel, groups, space, unit, rows,...  22.5 us
    pallas_call x1, Pallas kernels, per_device(): pl.pallas_call(finish_kernel, out_shape=tuple((jax.ShapeDtypeStruct(*x) f...  1.08 us

profile of v4, /device:TPU:16, one launch (start us, length us, event | category | flops | bytes accessed | tf_op | source)
XLA Modules:
  0.0 24.9 jit_solution(7767953361082891912)
XLA Ops:
  1.3 22.5 %main.1 = (bf16[40,128,128]{2,1,0:T(8,128)(2,1)S(1)}, f32[432,128]{1,0:T(8,128)S(1)}) custom-call(s32[1,1]{1,0:T(1,128)S(6)} %copy.8.counts_far, s32[16,27]{1,0:T(8,128)} %bitcast.7, bf16[16,128,128]{2,1,0:T(8,128)(2,1)} %bitcast.5, bf16[27,128,128]{2,1,0:T(8,128)(2,1)} %w_far.1, bf16[16,128,128]{2,1,0:T(8,128)(2,1)} %bitcast.6), custom_call_target="tpu_custom_call" | custom-call | tf_op jit(solution)/shard_map/main/pallas_call | solution.py:475
  23.8 1.1 %finish.1 = (bf16[16,128,128]{2,1,0:T(8,128)(2,1)}, bf16[16,128,128]{2,1,0:T(8,128)(2,1)}, f32[432,128]{1,0:T(8,128)}) custom-call(bf16[40,128,128]{2,1,0:T(8,128)(2,1)S(1)} %get-tuple-element.8.fin, f32[432,128]{1,0:T(8,128)S(1)} %get-tuple-element.9.wg_in), custom_call_target="tpu_custom_call" | custom-call | tf_op jit(solution)/shard_map/finish/pallas_call | solution.py:513

commit v5 on v4

--- a/solution.py
+++ b/solution.py
@@ -42,7 +42,7 @@
     z_peers = [(g, ((z + d) % half) * 2 + c) for d in range(1, half)]
     copy = pltpu.make_async_copy
     far = 3 - 2 * (g % 2)
-    turns = [far, 2, 4 - far] if groups == 4 else list(range(1, groups))
+    turns = [far, 4 - far, 2] if groups == 4 else list(range(1, groups))
 
     barrier = pltpu.get_barrier_semaphore()
     fixed = [partner] + grp_peers + z_peers

time: 25.1 us -> 25.1 us (level)
  no operation moved by 1% of the time
where the time goes in v5:
time: 25.1 us; the launch traced here: 24.8 us
  Pallas kernels  23.6 us (94%)
  between operations  1.29 us (5%)
    pallas_call x1, Pallas kernels, per_device(): pl.pallas_call(functools.partial(main_kernel, groups, space, unit, rows,...  22.5 us
    pallas_call x1, Pallas kernels, per_device(): pl.pallas_call(finish_kernel, out_shape=tuple((jax.ShapeDtypeStruct(*x) f...  1.08 us

profile of v5, /device:TPU:16, one launch (start us, length us, event | category | flops | bytes accessed | tf_op | source)
XLA Modules:
  0.0 24.8 jit_solution(11400866805905708196)
XLA Ops:
  1.3 22.5 %main.1 = (bf16[40,128,128]{2,1,0:T(8,128)(2,1)S(1)}, f32[432,128]{1,0:T(8,128)S(1)}) custom-call(s32[1,1]{1,0:T(1,128)S(6)} %copy.8.counts_far, s32[16,27]{1,0:T(8,128)} %bitcast.7, bf16[16,128,128]{2,1,0:T(8,128)(2,1)} %bitcast.5, bf16[27,128,128]{2,1,0:T(8,128)(2,1)} %w_far.1, bf16[16,128,128]{2,1,0:T(8,128)(2,1)} %bitcast.6), custom_call_target="tpu_custom_call" | custom-call | tf_op jit(solution)/shard_map/main/pallas_call | solution.py:475
  23.8 1.1 %finish.1 = (bf16[16,128,128]{2,1,0:T(8,128)(2,1)}, bf16[16,128,128]{2,1,0:T(8,128)(2,1)}, f32[432,128]{1,0:T(8,128)}) custom-call(bf16[40,128,128]{2,1,0:T(8,128)(2,1)S(1)} %get-tuple-element.8.fin, f32[432,128]{1,0:T(8,128)S(1)} %get-tuple-element.9.wg_in), custom_call_target="tpu_custom_call" | custom-call | tf_op jit(solution)/shard_map/finish/pallas_call | solution.py:513

commit v6 on v4

--- a/solution.py
+++ b/solution.py
@@ -10,7 +10,7 @@
 H = 4
 WIDE = 2 * H
 SPAN = 7
-BUILT, PAUSED = 11, 13
+BUILT, PAUSED = 12, 14
 BF16, F32 = jnp.bfloat16, jnp.float32
 VMEM = pl.BlockSpec(memory_space=pltpu.VMEM)
 FAR = pl.BlockSpec(memory_space=pl.ANY)

time: 25.1 us -> 25.1 us (level)
  no operation moved by 1% of the time
where the time goes in v6:
time: 25.1 us; the launch traced here: 24.9 us
  Pallas kernels  23.6 us (94%)
  between operations  1.29 us (5%)
    pallas_call x1, Pallas kernels, per_device(): pl.pallas_call(functools.partial(main_kernel, groups, space, unit, rows,...  22.5 us
    pallas_call x1, Pallas kernels, per_device(): pl.pallas_call(finish_kernel, out_shape=tuple((jax.ShapeDtypeStruct(*x) f...  1.08 us

profile of v6, /device:TPU:16, one launch (start us, length us, event | category | flops | bytes accessed | tf_op | source)
XLA Modules:
  0.0 24.9 jit_solution(12118846851600889215)
XLA Ops:
  1.3 22.5 %main.1 = (bf16[40,128,128]{2,1,0:T(8,128)(2,1)S(1)}, f32[432,128]{1,0:T(8,128)S(1)}) custom-call(s32[1,1]{1,0:T(1,128)S(6)} %copy.8.counts_far, s32[16,27]{1,0:T(8,128)} %bitcast.7, bf16[16,128,128]{2,1,0:T(8,128)(2,1)} %bitcast.5, bf16[27,128,128]{2,1,0:T(8,128)(2,1)} %w_far.1, bf16[16,128,128]{2,1,0:T(8,128)(2,1)} %bitcast.6), custom_call_target="tpu_custom_call" | custom-call | tf_op jit(solution)/shard_map/main/pallas_call | solution.py:475
  23.8 1.1 %finish.1 = (bf16[16,128,128]{2,1,0:T(8,128)(2,1)}, bf16[16,128,128]{2,1,0:T(8,128)(2,1)}, f32[432,128]{1,0:T(8,128)}) custom-call(bf16[40,128,128]{2,1,0:T(8,128)(2,1)S(1)} %get-tuple-element.8.fin, f32[432,128]{1,0:T(8,128)S(1)} %get-tuple-element.9.wg_in), custom_call_target="tpu_custom_call" | custom-call | tf_op jit(solution)/shard_map/finish/pallas_call | solution.py:513
